TPU v7x, 32 devices: a whole 2x2x4 slice. The times are simulated.
32 devices in a mesh: date: 2 (over y), trade: 8 (over z, x), path: 2 (over core).
Axes of the slice: x: 2, y: 2, z: 4, core: 2. Of those that a mesh axis runs over, the one named last changes fastest.
Arguments:
- basis_values: bfloat16 [2048, 512], P(('date', 'path')), parts along dimension 0, may hold values from -6 to 6
- coefficients: bfloat16 [2560, 512], P(('date', 'trade')), parts along dimension 0, may hold values from -0.25 to 0.25
- trade_cpty: int32 [1280], P('trade'), may hold values from 0 to 127, as said below
- trade_bucket: int32 [1280], P('trade'), may hold values from 0 to 127
- risk_weights: float32 [128], replicated, may hold values from 0.5 to 2
- correlation: float32 [128, 128], replicated, may hold values from 0 to 1, as said below
- funding_spread: float32 [128], P('trade'), may hold values from 0.5 to 2
Outputs:
- margin: float32 [128, 2048], P('trade', ('date', 'path')), parts along dimension 1
- basis_adjoint: bfloat16 [2048, 512], P(('date', 'path')), parts along dimension 0
There are 2 independent parts, one for each index of `date`. A program takes and returns all parts, laid end to end along the dimension named above; an argument that names none is the same for every part. Nothing has to cross between parts.
Inputs may be any that keep to these rules, and one draw needn't show every extreme that they name: `trade_cpty`: counterparty c belongs to owner block c // 16. Among the trades of one device, at most 40 belong to counterparties of one owner block; in every draw one owner block receives exactly 40 from every device. Counterparties differ in size. `correlation`: symmetric positive definite with unit diagonal; smallest eigenvalue at least 0.01; entries positive.
All inputs are finite; a program needn't handle non-finite values.
Results may differ from a plain program's by a relative error of at most 0.0034.
Values may be sent and summed in bfloat16 or wider, within the bound.
No kernel may reach another device: no remote copies, remote signals or barrier semaphores. Data moves between devices by JAX's collectives and lax.ppermute only.
A program may use at most 64 MiB of HBM per device.

v0:
```python
import jax
import jax.numpy as jnp
from jax import lax
from jax.sharding import PartitionSpec as P


def margin_terms(arrived, got_codes, risk_weights, correlation, funding_spread):
    path_rows = arrived.shape[0]
    cpty_count = funding_spread.shape[0]
    bucket_count = risk_weights.shape[0]
    is_filled = got_codes >= 0
    column_ids = jnp.arange(cpty_count * bucket_count, dtype=jnp.int32)
    hot_table = (got_codes[:, None] == column_ids[None, :]).astype(jnp.bfloat16)
    bucket_sums = jnp.dot(arrived, hot_table, preferred_element_type=jnp.float32)
    weighted = (
        bucket_sums.reshape(path_rows, cpty_count, bucket_count) * risk_weights[None, None, :]
    )
    rho_w = jnp.einsum("pcb,db->pcd", weighted, correlation, precision=lax.Precision.HIGHEST)
    margin_now = jnp.sqrt(jnp.sum(weighted * rho_w, axis=2) + 1e-06)
    sens_bar = (
        funding_spread[None, :, None] * risk_weights[None, None, :] * rho_w / margin_now[:, :, None]
    )
    flat_bar = sens_bar.reshape(path_rows, cpty_count * bucket_count)
    safe_codes = jnp.where(is_filled, got_codes, 0)
    slot_bar = jnp.take(flat_bar, safe_codes, axis=1) * is_filled[None, :].astype(jnp.float32)
    return (margin_now, slot_bar.astype(jnp.bfloat16))


def body(
    basis_values, coefficients, trade_cpty, trade_bucket, risk_weights, correlation, funding_spread
):
    owners = lax.axis_size("trade")
    per_device = coefficients.shape[0]
    capacity = max(2, 2 * per_device // owners)
    slot_total = owners * capacity
    cpty_count = funding_spread.shape[0]
    bucket_count = risk_weights.shape[0]
    path_rows = basis_values.shape[0]
    owner_of = trade_cpty // cpty_count
    trade_code = trade_cpty % cpty_count * bucket_count + trade_bucket
    position = jnp.arange(per_device, dtype=jnp.int32)
    same_owner = owner_of[:, None] == owner_of[None, :]
    earlier = position[None, :] < position[:, None]
    rank_in = jnp.sum((same_owner & earlier).astype(jnp.int32), axis=1)
    slot_index = owner_of * capacity + rank_in
    codes_out = jnp.full((slot_total,), -1, jnp.int32).at[slot_index].set(trade_code)
    got_codes = lax.all_to_all(codes_out, "trade", split_axis=0, concat_axis=0, tiled=True)
    delta_rows = lax.dot_general(
        basis_values, coefficients, (((1,), (1,)), ((), ())), preferred_element_type=jnp.float32
    ).astype(jnp.bfloat16)
    outgoing = jnp.zeros((path_rows, slot_total), jnp.bfloat16).at[:, slot_index].set(delta_rows)
    arrived = lax.all_to_all(outgoing, "trade", split_axis=1, concat_axis=1, tiled=True)
    margin_now, slot_bar = margin_terms(
        arrived, got_codes, risk_weights, correlation, funding_spread
    )
    returned = lax.all_to_all(slot_bar, "trade", split_axis=1, concat_axis=1, tiled=True)
    delta_bar = returned[:, slot_index]
    partial_adj = jnp.dot(delta_bar, coefficients, preferred_element_type=jnp.float32)
    basis_adjoint = lax.psum(partial_adj, "trade").astype(jnp.bfloat16)
    return (margin_now.T, basis_adjoint)


def solution(mesh):
    placed = (
        P(("date", "path"), None),
        P(("date", "trade"), None),
        P("trade"),
        P("trade"),
        P(),
        P(),
        P("trade"),
    )
    return jax.shard_map(
        body,
        mesh=mesh,
        in_specs=placed,
        out_specs=(P("trade", ("date", "path")), P(("date", "path"), None)),
        check_vma=False,
    )
```

profile of v0, /device:TPU:0, one launch (start us, length us, event | category | flops | bytes accessed | tf_op | source)
XLA Modules:
  0.0 130.3 jit_solution(14144373721821639996)
XLA Ops:
  0.6 0.0 copy-start
  0.6 0.8 fusion.14
  1.4 0.2 convert_reduce_fusion
  1.6 1.1 scatter_custom_fusion.1
  2.7 0.7 all_to_all.25
  3.4 7.3 %all-to-all-start.1 = ((s32[8,40,1]{1,2,0:T(1,128)}), s32[8,40,1]{1,2,0:T(1,128)S(1)}, u32[]{:S(2)}, u32[]{:S(2)}) async-start(s32[8,40,1]{1,2,0:T(1,128)} %all_to_all.25), calls=%async_computation.1 | async-start | bytes 8192 | tf_op jit(solution)/shard_map/all_to_all | solution.py:47
  10.6 0.0 copy-done
  10.7 1.2 fusion.7
  11.9 0.0 copy-start.2
  11.9 0.0 copy-start.3
  11.9 1.9 %scatter_custom_fusion = bf16[512,320]{0,1:T(8,128)(2,1)} fusion(s32[160]{0:T(256)S(1)} %compare_select_fusion.4, bf16[160,512]{1,0:T(8,128)(2,1)S(1)} %fusion.7, bf16[]{:T(256)} %constant.45.clone.1), kind=kCustom, calls=%fused_computation.18 | custom fusion | bytes 327682 | tf_op jit(solution)/shard_map/scatter | solution.py:51
  13.8 3.2 %all-to-all-done.1 = s32[8,40,1]{1,2,0:T(1,128)S(1)} async-done(((s32[8,40,1]{1,2,0:T(1,128)}), s32[8,40,1]{1,2,0:T(1,128)S(1)}, u32[]{:S(2)}, u32[]{:S(2)}) %all-to-all-start.1) | async-done | bytes 1312 | tf_op jit(solution)/shard_map/all_to_all | solution.py:47
  17.0 3.4 %all-to-all-start = ((bf16[512,8,40]{0,2,1:T(8,128)(2,1)}), bf16[512,8,40]{0,2,1:T(8,128)(2,1)S(1)}, u32[]{:S(2)}, u32[]{:S(2)}) async-start(bf16[512,8,40]{0,2,1:T(8,128)(2,1)} %bitcast.1), calls=%async_computation | async-start | bytes 655360 | tf_op jit(solution)/shard_map/all_to_all | solution.py:52
  20.5 0.7 broadcast_multiply_fusion
  21.2 0.5 broadcast.164
  21.7 0.7 reduce.7
  22.4 0.1 eq.51
  22.5 0.1 all_to_all.27
  22.6 6.9 %all-to-all-done = bf16[512,8,40]{0,2,1:T(8,128)(2,1)S(1)} async-done(((bf16[512,8,40]{0,2,1:T(8,128)(2,1)}), bf16[512,8,40]{0,2,1:T(8,128)(2,1)S(1)}, u32[]{:S(2)}, u32[]{:S(2)}) %all-to-all-start) | async-done | bytes 327712 | tf_op jit(solution)/shard_map/all_to_all | solution.py:52
  29.6 1.4 %fusion.2 = f32[512,16,128]{0,2,1:T(8,128)S(1)} fusion(bf16[512,320,1]{0,1,2:T(8,128)(2,1)S(1)} %bitcast.29, s32[16,128]{1,0:T(8,128)S(1)} %multiply_add_fusion, s32[320]{0:T(512)S(1)} %eq.51), kind=kOutput, calls=%fused_computation.8 | convolution fusion | flops 671744000 | bytes 4531456 | tf_op jit(solution)/shard_map/dot_general | solution.py:14
  30.9 0.0 copy-done.2
  30.9 0.0 copy-done.3
  31.0 5.5 %multiply_reduce_fusion = (f32[512,16]{0,1:T(8,128)S(1)}, f32[512,16,128]{0,2,1:T(8,128)S(1)}) fusion(f32[512,16,128]{0,2,1:T(8,128)S(1)} %fusion.2, f32[128]{0:T(128)S(1)} %copy-done.3, f32[128,128]{1,0:T(8,128)S(1)} %copy-done.2), kind=kOutput, calls=%fused_computation.5 | convolution fusion | flops 1614798848 | bytes 8487424 | tf_op jit(solution)/shard_map/pcb,db->pcd/dot_general | solution.py:18
  36.4 0.6 add_sqrt_fusion
  37.1 2.4 %multiply_divide_fusion = f32[512,16,128]{0,2,1:T(8,128)} fusion(f32[512,16,128]{0,2,1:T(8,128)S(1)} %get-tuple-element.9, f32[512,16]{0,1:T(8,128)S(1)} %get-tuple-element.2, f32[16,128]{1,0:T(8,128)S(1)} %broadcast_multiply_fusion), kind=kLoop, calls=%fused_computation.4 | loop fusion | flops 2097152 | bytes 8429568 | tf_op jit(solution)/shard_map/div | solution.py:21
  39.5 0.0 copy-start.1
  39.5 4.3 %gather_fusion = f32[320,512]{1,0:T(8,128)S(1)} fusion(f32[512,2048]{0,1:T(8,128)} %bitcast.26, s32[1024]{0:T(1024)S(1)} %pad_clamp_fusion.1), kind=kCustom, calls=%fused_computation | custom fusion | bytes 1312000 | tf_op jit(solution)/shard_map/jit(_take)/gather | solution.py:25
  43.8 0.9 multiply_convert_fusion
  44.7 3.6 %all-to-all-start.2 = ((bf16[512,8,40]{0,2,1:T(8,128)(2,1)}), bf16[512,8,40]{0,2,1:T(8,128)(2,1)S(1)}, u32[]{:S(2)}, u32[]{:S(2)}) async-start(bf16[512,8,40]{0,2,1:T(8,128)(2,1)} %multiply_convert_fusion), calls=%async_computation.2 | async-start | bytes 655360 | tf_op jit(solution)/shard_map/all_to_all | solution.py:56
  48.3 9.6 %all-to-all-done.2 = bf16[512,8,40]{0,2,1:T(8,128)(2,1)S(1)} async-done(((bf16[512,8,40]{0,2,1:T(8,128)(2,1)}), bf16[512,8,40]{0,2,1:T(8,128)(2,1)S(1)}, u32[]{:S(2)}, u32[]{:S(2)}) %all-to-all-start.2) | async-done | bytes 327712 | tf_op jit(solution)/shard_map/all_to_all | solution.py:56
  57.9 0.9 gather_fusion.1
  58.8 0.0 copy-done.1
  58.8 0.3 fusion.18
  59.2 71.2 %all-reduce.1 = bf16[512,512]{1,0:T(8,128)(2,1)} all-reduce(f32[512,512]{1,0:T(8,128)S(1)} %fusion.18), channel_id=1, replica_groups=mesh['date'=2,'trade'=8,'path'=2] {'trade'}, use_global_device_ids=true, to_apply=%region_4.5 | all-reduce | flops 262144 | bytes 1572864 | tf_op jit(solution)/shard_map/psum | solution.py:59
  (6 shorter events, 0.1 us)
Async XLA Ops:
  0.6 10.0 %copy-start = (bf16[512,512]{1,0:T(8,128)(2,1)S(1)}, bf16[512,512]{1,0:T(8,128)(2,1)}, u32[]{:S(2)}) copy-start(bf16[512,512]{1,0:T(8,128)(2,1)} %param.7) | copy-start | bytes 1572868
  3.4 13.6 %all-to-all-start.1 = ((s32[8,40,1]{1,2,0:T(1,128)}), s32[8,40,1]{1,2,0:T(1,128)S(1)}, u32[]{:S(2)}, u32[]{:S(2)}) async-start(s32[8,40,1]{1,2,0:T(1,128)} %all_to_all.25), calls=%async_computation.1 | async-start | bytes 8192 | tf_op jit(solution)/shard_map/all_to_all | solution.py:47
  11.9 19.0 %copy-start.2 = (f32[128,128]{1,0:T(8,128)S(1)}, f32[128,128]{1,0:T(8,128)}, u32[]{:S(2)}) copy-start(f32[128,128]{1,0:T(8,128)} %param.12) | copy-start | bytes 196612
  11.9 19.0 %copy-start.3 = (f32[128]{0:T(128)S(1)}, f32[128]{0:T(128)}, u32[]{:S(2)}) copy-start(f32[128]{0:T(128)} %param.11) | copy-start | bytes 1540
  17.0 12.5 %all-to-all-start = ((bf16[512,8,40]{0,2,1:T(8,128)(2,1)}), bf16[512,8,40]{0,2,1:T(8,128)(2,1)S(1)}, u32[]{:S(2)}, u32[]{:S(2)}) async-start(bf16[512,8,40]{0,2,1:T(8,128)(2,1)} %bitcast.1), calls=%async_computation | async-start | bytes 655360 | tf_op jit(solution)/shard_map/all_to_all | solution.py:52
  39.5 19.3 %copy-start.1 = (bf16[160,512]{1,0:T(8,128)(2,1)S(1)}, bf16[160,512]{1,0:T(8,128)(2,1)}, u32[]{:S(2)}) copy-start(bf16[160,512]{1,0:T(8,128)(2,1)} %param.8) | copy-start | bytes 491524
  44.7 13.2 %all-to-all-start.2 = ((bf16[512,8,40]{0,2,1:T(8,128)(2,1)}), bf16[512,8,40]{0,2,1:T(8,128)(2,1)S(1)}, u32[]{:S(2)}, u32[]{:S(2)}) async-start(bf16[512,8,40]{0,2,1:T(8,128)(2,1)} %multiply_convert_fusion), calls=%async_computation.2 | async-start | bytes 655360 | tf_op jit(solution)/shard_map/all_to_all | solution.py:56
where the time goes:
time: 131 us; the launch traced here: 130 us
  blocking collectives  71.2 us (54%)
  waiting for transfers between devices  19.8 us (15%)
  starting transfers between devices  14.3 us (11%)
  local copies, waits for them, and re-layouts  9.56 us (7%)
  matrix products  8.42 us (6%)
  other arithmetic  6.37 us (5%)
    psum x1, blocking collectives, body(): basis_adjoint = lax.psum(partial_adj, 'trade').astype(jnp.bfloat16)  71.2 us
    all_to_all x1, waiting for transfers between devices, body(): lax.all_to_all(slot_bar, 'trade', split_axis=1, concat_axis=1, tiled=True)  9.6 us
    all_to_all x1, starting transfers between devices, body(): lax.all_to_all(codes_out, 'trade', split_axis=0, concat_axis=0, tiled=True)  7.25 us
    all_to_all x1, waiting for transfers between devices, body(): lax.all_to_all(outgoing, 'trade', split_axis=1, concat_axis=1, tiled=True)  6.93 us
    dot_general x1, matrix products, margin_terms(): jnp.einsum('pcb,db->pcd', weighted, correlation, precision=lax.Precision....  5.47 us
    gather x1, local copies, waits for them, and re-layouts, margin_terms(): jnp.take(flat_bar, safe_codes, axis=1)  4.27 us
    all_to_all x1, starting transfers between devices, body(): lax.all_to_all(slot_bar, 'trade', split_axis=1, concat_axis=1, tiled=True)  3.6 us
    all_to_all x1, starting transfers between devices, body(): lax.all_to_all(outgoing, 'trade', split_axis=1, concat_axis=1, tiled=True)  3.43 us
  transfers between devices with their start and end apart: 3, of which 3 were waited for; matrix products, arithmetic and copies ran while one was open for 4% of the time, Pallas kernels for 0%

commit v1 on v0

--- a/solution.py
+++ b/solution.py
@@ -56,7 +56,7 @@
     returned = lax.all_to_all(slot_bar, "trade", split_axis=1, concat_axis=1, tiled=True)
     delta_bar = returned[:, slot_index]
     partial_adj = jnp.dot(delta_bar, coefficients, preferred_element_type=jnp.float32)
-    basis_adjoint = lax.psum(partial_adj, "trade").astype(jnp.bfloat16)
+    basis_adjoint = jnp.sum(lax.all_gather(partial_adj, "trade"), axis=0).astype(jnp.bfloat16)
     return (margin_now.T, basis_adjoint)
 
 

time: 131 us -> 204 us (1.56)
  waiting for transfers between devices: 19.8 us -> 144 us
  blocking collectives: 71.2 us -> 0 us
  between operations: 0.77 us -> 14.2 us
  other arithmetic: 6.37 us -> 11.7 us
    all_gather x0 -> x1, waiting for transfers between devices: none -> 124 us  [body(): lax.all_gather(partial_adj, 'trade')]
    psum x1 -> x0, blocking collectives: 71.2 us -> none  [body(): basis_adjoint = lax.psum(partial_adj, 'trade').astype(jnp.bfloat16)]
    reduce_sum x0 -> x1, other arithmetic: none -> 5.33 us  [body(): jnp.sum(lax.all_gather(partial_adj, 'trade'), axis=0).astype(jnp.bfloat16)]
  transfers between devices with their start and end apart: 3 -> 4, of which waited for: 3 -> 4; matrix products, arithmetic and copies ran while one was open for 4% -> 3% of each run, Pallas kernels for 0% -> 0%
where the time goes in v1:
time: 204 us; the launch traced here: 203 us
  waiting for transfers between devices  144 us (71%)
  starting transfers between devices  14.3 us (7%)
  between operations  14.2 us (7%)
  other arithmetic  11.7 us (6%)
  local copies, waits for them, and re-layouts  9.56 us (5%)
  matrix products  9.48 us (5%)
    all_gather x1, waiting for transfers between devices, body(): lax.all_gather(partial_adj, 'trade')  124 us
    all_to_all x1, waiting for transfers between devices, body(): lax.all_to_all(slot_bar, 'trade', split_axis=1, concat_axis=1, tiled=True)  9.56 us
    all_to_all x1, starting transfers between devices, body(): lax.all_to_all(codes_out, 'trade', split_axis=0, concat_axis=0, tiled=True)  7.25 us
    all_to_all x1, waiting for transfers between devices, body(): lax.all_to_all(outgoing, 'trade', split_axis=1, concat_axis=1, tiled=True)  6.93 us
    dot_general x1, matrix products, margin_terms(): jnp.einsum('pcb,db->pcd', weighted, correlation, precision=lax.Precision....  5.47 us
    reduce_sum x1, other arithmetic, body(): jnp.sum(lax.all_gather(partial_adj, 'trade'), axis=0).astype(jnp.bfloat16)  5.33 us
    gather x1, local copies, waits for them, and re-layouts, margin_terms(): jnp.take(flat_bar, safe_codes, axis=1)  4.27 us
  transfers between devices with their start and end apart: 4, of which 4 were waited for; matrix products, arithmetic and copies ran while one was open for 3% of the time, Pallas kernels for 0%

profile of v1, /device:TPU:0, one launch (start us, length us, event | category | flops | bytes accessed | tf_op | source)
XLA Modules:
  0.0 203.1 jit_solution(15023512614674162897)
XLA Ops:
  7.2 0.0 copy-start
  7.2 0.8 fusion.14
  7.9 0.2 convert_reduce_fusion
  8.1 1.1 scatter_custom_fusion.1
  9.2 0.7 all_to_all.25
  9.9 7.3 %all-to-all-start.1 = ((s32[8,40,1]{1,2,0:T(1,128)}), s32[8,40,1]{1,2,0:T(1,128)S(1)}, u32[]{:S(2)}, u32[]{:S(2)}) async-start(s32[8,40,1]{1,2,0:T(1,128)} %all_to_all.25), calls=%async_computation.1 | async-start | bytes 8192 | tf_op jit(solution)/shard_map/all_to_all | solution.py:47
  17.2 0.0 copy-done
  17.2 1.2 fusion.7
  18.4 0.0 copy-start.2
  18.4 0.0 copy-start.3
  18.5 1.9 scatter_custom_fusion
  20.3 3.2 %all-to-all-done.1 = s32[8,40,1]{1,2,0:T(1,128)S(1)} async-done(((s32[8,40,1]{1,2,0:T(1,128)}), s32[8,40,1]{1,2,0:T(1,128)S(1)}, u32[]{:S(2)}, u32[]{:S(2)}) %all-to-all-start.1) | async-done | bytes 1312 | tf_op jit(solution)/shard_map/all_to_all | solution.py:47
  23.6 3.4 %all-to-all-start = ((bf16[512,8,40]{0,2,1:T(8,128)(2,1)}), bf16[512,8,40]{0,2,1:T(8,128)(2,1)S(1)}, u32[]{:S(2)}, u32[]{:S(2)}) async-start(bf16[512,8,40]{0,2,1:T(8,128)(2,1)} %bitcast.1), calls=%async_computation | async-start | bytes 655360 | tf_op jit(solution)/shard_map/all_to_all | solution.py:52
  27.0 0.7 broadcast_multiply_fusion
  27.8 0.1 all_to_all.27
  27.8 0.5 broadcast.164
  28.4 0.7 reduce.7
  29.0 0.1 eq.51
  29.2 6.9 %all-to-all-done = bf16[512,8,40]{0,2,1:T(8,128)(2,1)S(1)} async-done(((bf16[512,8,40]{0,2,1:T(8,128)(2,1)}), bf16[512,8,40]{0,2,1:T(8,128)(2,1)S(1)}, u32[]{:S(2)}, u32[]{:S(2)}) %all-to-all-start) | async-done | bytes 327712 | tf_op jit(solution)/shard_map/all_to_all | solution.py:52
  36.1 1.4 fusion.2
  37.5 0.0 copy-done.2
  37.5 0.0 copy-done.3
  37.5 5.5 %multiply_reduce_fusion = (f32[512,16]{0,1:T(8,128)S(1)}, f32[512,16,128]{0,2,1:T(8,128)S(1)}) fusion(f32[512,16,128]{0,2,1:T(8,128)S(1)} %fusion.2, f32[128]{0:T(128)S(1)} %copy-done.3, f32[128,128]{1,0:T(8,128)S(1)} %copy-done.2), kind=kOutput, calls=%fused_computation.5 | convolution fusion | flops 1614798848 | bytes 8487424 | tf_op jit(solution)/shard_map/pcb,db->pcd/dot_general | solution.py:18
  43.0 0.6 add_sqrt_fusion
  43.6 2.4 %multiply_divide_fusion = f32[512,16,128]{0,2,1:T(8,128)} fusion(f32[512,16,128]{0,2,1:T(8,128)S(1)} %get-tuple-element.9, f32[512,16]{0,1:T(8,128)S(1)} %get-tuple-element.2, f32[16,128]{1,0:T(8,128)S(1)} %broadcast_multiply_fusion), kind=kLoop, calls=%fused_computation.4 | loop fusion | flops 2097152 | bytes 8429568 | tf_op jit(solution)/shard_map/div | solution.py:21
  46.0 0.0 copy-start.1
  46.0 4.3 %gather_fusion = f32[320,512]{1,0:T(8,128)S(1)} fusion(f32[512,2048]{0,1:T(8,128)} %bitcast.29, s32[1024]{0:T(1024)S(1)} %pad_clamp_fusion.1), kind=kCustom, calls=%fused_computation | custom fusion | bytes 1312000 | tf_op jit(solution)/shard_map/jit(_take)/gather | solution.py:25
  50.3 0.9 multiply_convert_fusion
  51.2 3.6 %all-to-all-start.2 = ((bf16[512,8,40]{0,2,1:T(8,128)(2,1)}), bf16[512,8,40]{0,2,1:T(8,128)(2,1)S(1)}, u32[]{:S(2)}, u32[]{:S(2)}) async-start(bf16[512,8,40]{0,2,1:T(8,128)(2,1)} %multiply_convert_fusion), calls=%async_computation.2 | async-start | bytes 655360 | tf_op jit(solution)/shard_map/all_to_all | solution.py:56
  54.8 0.0 all-gather.3.cloned.1.call-start
  54.9 9.6 %all-to-all-done.2 = bf16[512,8,40]{0,2,1:T(8,128)(2,1)S(1)} async-done(((bf16[512,8,40]{0,2,1:T(8,128)(2,1)}), bf16[512,8,40]{0,2,1:T(8,128)(2,1)S(1)}, u32[]{:S(2)}, u32[]{:S(2)}) %all-to-all-start.2) | async-done | bytes 327712 | tf_op jit(solution)/shard_map/all_to_all | solution.py:56
  64.4 0.9 gather_fusion.1
  65.3 0.0 copy-done.1
  65.3 1.4 fusion.18
  66.8 0.0 all-gather.3.cloned.1.call-update
  66.8 124.2 %all-gather.3.cloned.1.call-done = f32[4096,512]{1,0:T(8,128)} async-done(((f32[512,512]{1,0:T(8,128)}), f32[4096,512]{1,0:T(8,128)}) %all-gather.3.cloned.1.call-update) | async-done | bytes 8388624 | tf_op jit(solution)/shard_map/all_gather | solution.py:59
  191.0 5.3 %reduce_sum.29 = bf16[512,512]{1,0:T(8,128)(2,1)} reduce(f32[8,512,512]{2,1,0:T(8,128)} %bitcast.31, f32[]{:T(128)} %constant.55.clone.1), dimensions={0}, to_apply=%region_4.5 | reduce | flops 1835008 | bytes 8912900 | tf_op jit(solution)/shard_map/reduce_sum | solution.py:59
  (6 shorter events, 0.1 us)
Async XLA Ops:
  7.2 10.0 %copy-start = (bf16[512,512]{1,0:T(8,128)(2,1)S(1)}, bf16[512,512]{1,0:T(8,128)(2,1)}, u32[]{:S(2)}) copy-start(bf16[512,512]{1,0:T(8,128)(2,1)} %param.7) | copy-start | bytes 1572868
  9.9 13.6 %all-to-all-start.1 = ((s32[8,40,1]{1,2,0:T(1,128)}), s32[8,40,1]{1,2,0:T(1,128)S(1)}, u32[]{:S(2)}, u32[]{:S(2)}) async-start(s32[8,40,1]{1,2,0:T(1,128)} %all_to_all.25), calls=%async_computation.1 | async-start | bytes 8192 | tf_op jit(solution)/shard_map/all_to_all | solution.py:47
  18.4 19.0 %copy-start.2 = (f32[128,128]{1,0:T(8,128)S(1)}, f32[128,128]{1,0:T(8,128)}, u32[]{:S(2)}) copy-start(f32[128,128]{1,0:T(8,128)} %param.12) | copy-start | bytes 196612
  18.4 19.0 %copy-start.3 = (f32[128]{0:T(128)S(1)}, f32[128]{0:T(128)}, u32[]{:S(2)}) copy-start(f32[128]{0:T(128)} %param.11) | copy-start | bytes 1540
  23.6 12.5 %all-to-all-start = ((bf16[512,8,40]{0,2,1:T(8,128)(2,1)}), bf16[512,8,40]{0,2,1:T(8,128)(2,1)S(1)}, u32[]{:S(2)}, u32[]{:S(2)}) async-start(bf16[512,8,40]{0,2,1:T(8,128)(2,1)} %bitcast.1), calls=%async_computation | async-start | bytes 655360 | tf_op jit(solution)/shard_map/all_to_all | solution.py:52
  46.0 19.3 %copy-start.1 = (bf16[160,512]{1,0:T(8,128)(2,1)S(1)}, bf16[160,512]{1,0:T(8,128)(2,1)}, u32[]{:S(2)}) copy-start(bf16[160,512]{1,0:T(8,128)(2,1)} %param.8) | copy-start | bytes 491524
  51.2 13.2 %all-to-all-start.2 = ((bf16[512,8,40]{0,2,1:T(8,128)(2,1)}), bf16[512,8,40]{0,2,1:T(8,128)(2,1)S(1)}, u32[]{:S(2)}, u32[]{:S(2)}) async-start(bf16[512,8,40]{0,2,1:T(8,128)(2,1)} %multiply_convert_fusion), calls=%async_computation.2 | async-start | bytes 655360 | tf_op jit(solution)/shard_map/all_to_all | solution.py:56
  54.8 136.2 %all-gather.3.cloned.1.call-start = ((), (), s32[]{:S(2)}) async-start(), calls=%async_computation.3 | async-start | bytes 9437184 | tf_op jit(solution)/shard_map/all_gather | solution.py:59
Sparse Core Ops, SparseCore 0:
  66.9 124.0 all-gather.2
